TPU v7x, 32 devices: a whole 2x2x4 slice. The times are simulated.
32 devices in a mesh: grp: 2 (over y), blk: 4 (over z), sub: 2 (over x), pair: 2 (over core).
Axes of the slice: x: 2, y: 2, z: 4, core: 2. Of those that a mesh axis runs over, the one named last changes fastest.
Arguments:
- grad_volume: bfloat16 [16, 128, 8192], P(('grp', 'blk', 'sub'), 'pair'), parts along dimension 0, may hold values from -6 to 6
- query_feats: bfloat16 [16384, 1024], P(('grp', 'blk')), parts along dimension 0, may hold values from -6 to 6
- support_feats: bfloat16 [16, 128, 1024], P(('grp', 'blk', 'sub'), 'pair'), parts along dimension 0, may hold values from -6 to 6
- query_kernel: float32 [3, 3], replicated, may hold values from -2 to 2
- support_kernel: float32 [3, 3], replicated, may hold values from -2 to 2
Outputs:
- query_grad: float32 [16384, 1024], P(('grp', 'blk', 'sub', 'pair')), parts along dimension 0
- support_grad: float32 [16, 128, 1024], P(('grp', 'blk', 'sub'), 'pair'), parts along dimension 0
There are 2 independent parts, one for each index of `grp`. A program takes and returns all parts, laid end to end along the dimension named above; an argument that names none is the same for every part. Nothing has to cross between parts.
All inputs are finite; a program needn't handle non-finite values.
Results may differ from a plain program's by a relative error of at most 0.0029.
Values may be sent and summed in bfloat16 or wider, within the bound.
No kernel may reach another device: no remote copies, remote signals or barrier semaphores. Data moves between devices by JAX's collectives and lax.ppermute only.
A program may use at most 64 MiB of HBM per device.

v0:
```python
import math
import jax
import jax.numpy as jnp
from jax import lax
from jax.sharding import PartitionSpec as P

QW = 128
QH = 64


def extended(cells, sides, width):
    for axis, dim in sides:
        count = lax.axis_size(axis)
        ends = count - 1
        head = lax.slice_in_dim(cells, 0, width, axis=dim)
        tail = lax.slice_in_dim(cells, cells.shape[dim] - width, cells.shape[dim], axis=dim)
        cells = jnp.concatenate(
            [
                lax.ppermute(tail, axis, [(i, (i + 1) % count) for i in range(ends)]),
                cells,
                lax.ppermute(head, axis, [((i + 1) % count, i) for i in range(ends)]),
            ],
            axis=dim,
        )
    return cells


def shifted(value, axis, steps):
    count = lax.axis_size(axis)
    pairs = [(source, (source + steps) % count) for source in range(count)]
    return lax.ppermute(value, axis, pairs)


def query_pass(volume, kernel):
    planes, columns, queries = volume.shape
    grid = volume.astype(jnp.float32).reshape(planes, columns, QH, QW)
    padded = jnp.pad(grid, ((0, 0), (0, 0), (1, 1), (1, 1)))
    total = jnp.zeros_like(grid)
    for row_shift in range(3):
        for col_shift in range(3):
            total = (
                total
                + kernel[row_shift, col_shift]
                * padded[:, :, row_shift : row_shift + QH, col_shift : col_shift + QW]
            )
    return total.reshape(planes, columns, queries)


def support_pass(rimmed, kernel, planes, columns):
    total = jnp.zeros((planes, columns, rimmed.shape[2]), jnp.float32)
    for row_shift in range(3):
        for col_shift in range(3):
            total = total + kernel[row_shift, col_shift] * rimmed[
                row_shift : row_shift + planes, col_shift : col_shift + columns
            ].astype(jnp.float32)
    return total


def shards(grad_volume, query_feats, support_feats, query_kernel, support_kernel):
    planes, columns, queries = grad_volume.shape
    rimmed = extended(grad_volume, ((("blk", "sub"), 0), ("pair", 1)), 1)
    corr_grad = (
        query_pass(grad_volume, query_kernel)
        + support_pass(rimmed, support_kernel, planes, columns)
    ).astype(jnp.bfloat16)
    moved = lax.all_to_all(corr_grad, "blk", split_axis=2, concat_axis=0, tiled=True)
    cycle_size = lax.axis_size("blk")
    own_index = lax.axis_index("blk")
    tile_len = moved.shape[2]
    tiles = moved.reshape(cycle_size, planes, columns, tile_len)
    width = query_feats.shape[1]
    scale_factor = 1.0 / math.sqrt(width)

    def project(piece_index, feat_piece, acc_piece, count):
        whole_block = lax.dynamic_index_in_dim(tiles, piece_index, 0, keepdims=False)
        block = whole_block.reshape(planes * count, tile_len)
        feat_flat = feat_piece.reshape(planes * count, width)
        query_term = lax.dot_general(
            block, feat_flat, (((0,), (0,)), ((), ())), preferred_element_type=jnp.float32
        )
        acc_new = acc_piece + jnp.dot(
            block, query_feats, preferred_element_type=jnp.float32
        ).reshape(planes, count, width)
        return (query_term, acc_new)

    query_start = jnp.zeros((tile_len, width), jnp.float32)

    def turn_one(turn_index, carry):
        query_total, feat_piece, acc_piece = carry
        term_piece, acc_piece = project(
            (own_index - turn_index) % cycle_size, feat_piece, acc_piece, columns
        )
        feat_piece = shifted(feat_piece, "blk", 1)
        acc_piece = shifted(acc_piece, "blk", 1)
        return (query_total + term_piece, feat_piece, acc_piece)

    start = (query_start, support_feats, jnp.zeros((planes, columns, width), jnp.float32))
    query_total, feat_piece, support_total = lax.fori_loop(0, cycle_size, turn_one, start)
    query_grad = (
        lax.psum_scatter(query_total, ("sub", "pair"), scatter_dimension=0, tiled=True)
        * scale_factor
    )
    return (query_grad, support_total * scale_factor)


def solution(mesh):
    in_specs = (
        P(("grp", "blk", "sub"), "pair", None),
        P(("grp", "blk"), None),
        P(("grp", "blk", "sub"), "pair", None),
        P(),
        P(),
    )
    out_specs = (P(("grp", "blk", "sub", "pair"), None), P(("grp", "blk", "sub"), "pair", None))
    return jax.shard_map(shards, mesh=mesh, in_specs=in_specs, out_specs=out_specs, check_vma=False)
```

profile of v0, /device:TPU:0, one launch (start us, length us, event | category | flops | bytes accessed | tf_op | source)
XLA Modules:
  0.0 318.6 jit_solution(11927447084421412007)
XLA Ops:
  7.2 0.0 copy-start.3
  7.2 5.0 %collective-permute-start.2 = (bf16[1,64,8192]{2,1,0:T(8,128)(2,1)}, bf16[1,64,8192]{2,1,0:T(8,128)(2,1)S(1)}, u32[]{:S(2)}, u32[]{:S(2)}) collective-permute-start(bf16[1,64,8192]{2,1,0:T(8,128)(2,1)} %param.7), channel_id=1, source_target_pairs={{0,2},{2,4},{4,6},{6,8},{8,10},{10,12},{12,14},{1,3},{3,5},{5,7},{... | collective-permute-start | bytes 3145736 | tf_op jit(solution)/shard_map/ppermute | solution.py:19
  12.2 1.3 collective-permute-start.3
  13.5 1.7 fusion.33
  15.2 1.7 fusion.32
  16.9 40.4 %collective-permute-done.2 = bf16[1,64,8192]{2,1,0:T(8,128)(2,1)S(1)} collective-permute-done((bf16[1,64,8192]{2,1,0:T(8,128)(2,1)}, bf16[1,64,8192]{2,1,0:T(8,128)(2,1)S(1)}, u32[]{:S(2)}, u32[]{:S(2)}) %collective-permute-start.2) | collective-permute-done | bytes 1048608 | tf_op jit(solution)/shard_map/ppermute | solution.py:19
  57.3 0.1 constant_dynamic-update-slice_fusion.2
  57.4 0.2 constant_dynamic-update-slice_fusion.1
  57.7 0.0 collective-permute-done.3
  57.7 0.1 constant_dynamic-update-slice_fusion
  57.8 0.2 fusion.31
  57.9 0.1 copy.21
  58.0 0.1 copy.22
  58.1 1.3 collective-permute-start.5
  59.4 3.0 collective-permute-start.4
  62.4 0.4 copy.23
  62.8 9.4 %fusion.23 = f32[1,64,64,128]{3,2,1,0:T(8,128)S(1)} fusion(f32[1,64,64,128]{3,2,1,0:T(8,128)S(1)} %bitcast.53, f32[]{:T(128)} %bitcast.8, f32[]{:T(128)} %bitcast.7, f32[]{:T(128)} %bitcast.6, f32[]{:T(128)} %bitcast.5, f32[]{:T(128)} %bitcast.4, f32[]{:T(128)} %bitcast.3, f32[]{:T(128)} %bitcast.2, f32[]{:T(128)} %bitcast.1, f32[]{:T(128)} %bitcast), kind=kLoop, calls=%fused_computation.35 | loop fusion | flops 8912896 | bytes 4194340 | tf_op jit(solution)/shard_map/add | solution.py:42
  72.3 1.5 reshape.56
  73.8 0.0 collective-permute-done.5
  73.8 0.1 copy.17
  73.9 0.0 collective-permute-done.4
  73.9 0.1 copy.15
  74.0 11.4 %fusion.14 = bf16[1,64,8192]{2,1,0:T(8,128)(2,1)S(1)} fusion(f32[1,64,8192]{2,1,0:T(8,128)} %reshape.56, bf16[1,64,8192]{2,1,0:T(8,128)(2,1)} %param.7, bf16[1,64,8192]{2,1,0:T(8,128)(2,1)} %copy-done.2, bf16[1,64,8192]{2,1,0:T(8,128)(2,1)S(1)} %collective-permute-done.2, bf16[3,1,8192]{2,1,0:T(2,128)(2,1)S(1)} %copy.17, bf16[3,64,8192]{2,1,0:T(8,128)(2,1)} %copy-done, ...), kind=kLoop, calls=%fused_computation.26 | loop fusion | flops 24117248 | bytes 9535524 | tf_op jit(solution)/shard_map/convert_element_type | solution.py:65
  85.4 6.8 %copy.18 = bf16[1,64,8192]{1,0,2:T(2,128)(2,1)} copy(bf16[1,64,8192]{2,1,0:T(8,128)(2,1)S(1)} %fusion.14) | data formatting | bytes 2097152 | tf_op jit(solution)/shard_map/convert_element_type | solution.py:65
  92.2 0.5 broadcast.17
  92.7 45.2 %reduce = bf16[8192,64]{1,0:T(8,128)(2,1)S(1)} reduce(bf16[8192,1,64]{2,1,0:T(2,128)(2,1)} %bitcast.51, bf16[]{:T(256)} %broadcast.17), dimensions={1}, to_apply=%bitcast.38.reduce_sub_computation | reduce | bytes 2097154
  138.0 2.7 reshape.60
  140.6 6.3 %all-to-all-start = ((bf16[4,2,65536]{2,1,0:T(2,128)(2,1)}), bf16[4,2,65536]{2,1,0:T(2,128)(2,1)S(1)}, u32[]{:S(2)}, u32[]{:S(2)}) async-start(bf16[4,2,65536]{2,1,0:T(2,128)(2,1)} %reshape.60), calls=%async_computation | async-start | bytes 2097152 | tf_op jit(solution)/shard_map/all_to_all | solution.py:66
  146.9 0.0 reduce-scatter.2.cloned.1.call-start
  146.9 25.3 %all-to-all-done = bf16[4,2,65536]{2,1,0:T(2,128)(2,1)S(1)} async-done(((bf16[4,2,65536]{2,1,0:T(2,128)(2,1)}), bf16[4,2,65536]{2,1,0:T(2,128)(2,1)S(1)}, u32[]{:S(2)}, u32[]{:S(2)}) %all-to-all-start) | async-done | bytes 1048608 | tf_op jit(solution)/shard_map/all_to_all | solution.py:66
  172.2 3.2 reshape.61
  175.4 8.2 %copy.19 = bf16[1,64,8192]{2,1,0:T(8,128)(2,1)S(1)} copy(bf16[1,64,8192]{1,0,2:T(2,128)(2,1)} %bitcast.52) | data formatting | bytes 2097152 | tf_op jit(solution)/shard_map/all_to_all | solution.py:66
  183.5 0.0 copy-start.1
  183.5 0.8 all_to_all.12
  184.3 0.6 copy.20
  185.0 52.0 %while.20 = (s32[]{:T(128)}, f32[2048,1024]{1,0:T(8,128)}, bf16[1,64,1024]{2,1,0:T(8,128)(2,1)S(1)}, f32[1,64,1024]{2,1,0:T(8,128)S(1)}, s32[]{:T(128)}, /*index...) while((s32[]{:T(128)}, f32[2048,1024]{1,0:T(8,128)}, ...), condition=%wide.region_1.2_spmd.clone, body=%wide.region_0.1_spmd.clone.sunk | while | flops 541130752 | bytes 23986536 | solution.py:98
  185.0 0.1 collective-permute-start
  185.1 3.0 fusion.44
  188.1 0.2 collective-permute-start.1
  188.4 4.5 %select_add_fusion.2 = f32[2048,1024]{1,0:T(8,128)} fusion(f32[2048,1024]{1,0:T(8,128)} %get-tuple-element.318, pred[]{:T(512)S(6)} %compare.5, bf16[4,1,64,2048]{3,2,1,0:T(8,128)(2,1)S(1)} %get-tuple-element.333, s32[]{:T(128)S(6)} %select_n.36, bf16[1,64,1024]{2,1,0:T(8,128)(2,1)S(1)} %copy.32), kind=kOutput, calls=%fused_computation.clone.1 | convolution fusion | flops 272629760 | bytes 17170436 | tf_op jit(solution)/shard_map/while/body/eval_jaxpr/dot_general | solution.py:78
  192.9 0.0 collective-permute-done
  192.9 4.6 %collective-permute-done.1 = f32[1,64,1024]{2,1,0:T(8,128)S(1)} collective-permute-done((f32[1,64,1024]{2,1,0:T(8,128)S(1)}, f32[1,64,1024]{2,1,0:T(8,128)S(1)}, u32[]{:S(2)}, u32[]{:S(2)}) %collective-permute-start.1) | collective-permute-done | bytes 262176 | tf_op jit(solution)/shard_map/while/body/eval_jaxpr/ppermute | solution.py:31
  197.4 0.1 collective-permute-start
  197.5 3.0 fusion.44
  200.6 0.2 collective-permute-start.1
  200.8 7.9 %select_add_fusion.2 = f32[2048,1024]{1,0:T(8,128)} fusion(f32[2048,1024]{1,0:T(8,128)} %get-tuple-element.318, pred[]{:T(512)S(6)} %compare.5, bf16[4,1,64,2048]{3,2,1,0:T(8,128)(2,1)S(1)} %get-tuple-element.333, s32[]{:T(128)S(6)} %select_n.36, bf16[1,64,1024]{2,1,0:T(8,128)(2,1)S(1)} %copy.32), kind=kOutput, calls=%fused_computation.clone.1 | convolution fusion | flops 272629760 | bytes 17170436 | tf_op jit(solution)/shard_map/while/body/eval_jaxpr/dot_general | solution.py:78
  208.6 0.0 collective-permute-done
  208.6 1.2 collective-permute-done.1
  209.9 1.3 collective-permute-start
  211.2 3.0 fusion.44
  214.2 2.4 collective-permute-start.1
  216.6 7.9 %select_add_fusion.2 = f32[2048,1024]{1,0:T(8,128)} fusion(f32[2048,1024]{1,0:T(8,128)} %get-tuple-element.318, pred[]{:T(512)S(6)} %compare.5, bf16[4,1,64,2048]{3,2,1,0:T(8,128)(2,1)S(1)} %get-tuple-element.333, s32[]{:T(128)S(6)} %select_n.36, bf16[1,64,1024]{2,1,0:T(8,128)(2,1)S(1)} %copy.32), kind=kOutput, calls=%fused_computation.clone.1 | convolution fusion | flops 272629760 | bytes 17170436 | tf_op jit(solution)/shard_map/while/body/eval_jaxpr/dot_general | solution.py:78
  224.5 0.0 collective-permute-done
  224.5 0.0 collective-permute-done.1
  224.5 0.1 collective-permute-start
  224.6 3.0 fusion.44
  227.6 1.4 collective-permute-start.1
  229.0 7.9 %select_add_fusion.2 = f32[2048,1024]{1,0:T(8,128)} fusion(f32[2048,1024]{1,0:T(8,128)} %get-tuple-element.318, pred[]{:T(512)S(6)} %compare.5, bf16[4,1,64,2048]{3,2,1,0:T(8,128)(2,1)S(1)} %get-tuple-element.333, s32[]{:T(128)S(6)} %select_n.36, bf16[1,64,1024]{2,1,0:T(8,128)(2,1)S(1)} %copy.32), kind=kOutput, calls=%fused_computation.clone.1 | convolution fusion | flops 272629760 | bytes 17170436 | tf_op jit(solution)/shard_map/while/body/eval_jaxpr/dot_general | solution.py:78
  236.9 0.0 collective-permute-done
  236.9 0.0 collective-permute-done.1
  236.9 0.0 reduce-scatter.2.cloned.1.call-update
  236.9 0.7 broadcast_multiply_fusion.1
  237.7 70.9 %reduce-scatter.2.cloned.1.call-done = f32[512,1024]{1,0:T(8,128)} async-done(((f32[2048,1024]{1,0:T(8,128)}), f32[512,1024]{1,0:T(8,128)}) %reduce-scatter.2.cloned.1.call-update) | async-done | bytes 2097168 | tf_op jit(solution)/shard_map/reduce_scatter | solution.py:100
  308.5 3.2 %broadcast_multiply_fusion = f32[512,1024]{1,0:T(8,128)} fusion(f32[512,1024]{1,0:T(8,128)} %reduce-scatter.2.cloned.1.call-done), kind=kLoop, calls=%fused_computation.45 | loop fusion | flops 524288 | bytes 4194304 | tf_op jit(solution)/shard_map/mul | solution.py:100
  (12 shorter events, 0.1 us)
Async XLA Ops:
  7.2 50.3 %copy-start.3 = (bf16[1,64,8192]{2,1,0:T(8,128)(2,1)S(1)}, bf16[1,64,8192]{2,1,0:T(8,128)(2,1)}, u32[]{:S(2)}) copy-start(bf16[1,64,8192]{2,1,0:T(8,128)(2,1)} %param.7) | copy-start | bytes 3145732
  7.2 50.2 %collective-permute-start.2 = (bf16[1,64,8192]{2,1,0:T(8,128)(2,1)}, bf16[1,64,8192]{2,1,0:T(8,128)(2,1)S(1)}, u32[]{:S(2)}, u32[]{:S(2)}) collective-permute-start(bf16[1,64,8192]{2,1,0:T(8,128)(2,1)} %param.7), channel_id=1, source_target_pairs={{0,2},{2,4},{4,6},{6,8},{8,10},{10,12},{12,14},{1,3},{3,5},{5,7},{... | collective-permute-start | bytes 3145736 | tf_op jit(solution)/shard_map/ppermute | solution.py:19
  12.2 45.5 %collective-permute-start.3 = (bf16[1,64,8192]{2,1,0:T(8,128)(2,1)}, bf16[1,64,8192]{2,1,0:T(8,128)(2,1)S(1)}, u32[]{:S(2)}, u32[]{:S(2)}) collective-permute-start(bf16[1,64,8192]{2,1,0:T(8,128)(2,1)} %param.7), channel_id=1, source_target_pairs={{2,0},{4,2},{6,4},{8,6},{10,8},{12,10},{14,12},{3,1},{5,3},{7,5},{... | collective-permute-start | bytes 3145736 | tf_op jit(solution)/shard_map/ppermute | solution.py:21
  57.7 5.1 %copy-start.2 = (bf16[1,64,8192]{2,1,0:T(8,128)(2,1)}, bf16[1,64,8192]{2,1,0:T(8,128)(2,1)S(1)}, u32[]{:S(2)}) copy-start(bf16[1,64,8192]{2,1,0:T(8,128)(2,1)S(1)} %collective-permute-done.3) | copy-start | bytes 3145732
  57.8 5.1 %copy-start = (bf16[3,64,8192]{2,1,0:T(8,128)(2,1)}, bf16[3,64,8192]{2,1,0:T(8,128)(2,1)S(1)}, u32[]{:S(2)}) copy-start(bf16[3,64,8192]{2,1,0:T(8,128)(2,1)S(1)} %constant_dynamic-update-slice_fusion) | copy-start | bytes 9437188
  58.1 15.7 %collective-permute-start.5 = (bf16[3,1,8192]{2,0,1:T(4,128)(2,1)S(1)}, bf16[3,1,8192]{2,0,1:T(4,128)(2,1)S(1)}, u32[]{:S(2)}, u32[]{:S(2)}) collective-permute-start(bf16[3,1,8192]{2,0,1:T(4,128)(2,1)S(1)} %copy.22), channel_id=1, source_target_pairs={{1,0},{3,2},{5,4},{7,6},{9,8},{11,10},{13,12},{15,14},{17,16},{19,... | collective-permute-start | bytes 147464 | tf_op jit(solution)/shard_map/ppermute | solution.py:21
  59.4 14.5 %collective-permute-start.4 = (bf16[3,1,8192]{2,0,1:T(4,128)(2,1)S(1)}, bf16[3,1,8192]{2,0,1:T(4,128)(2,1)S(1)}, u32[]{:S(2)}, u32[]{:S(2)}) collective-permute-start(bf16[3,1,8192]{2,0,1:T(4,128)(2,1)S(1)} %copy.21), channel_id=1, source_target_pairs={{0,1},{2,3},{4,5},{6,7},{8,9},{10,11},{12,13},{14,15},{16,17},{18,... | collective-permute-start | bytes 147464 | tf_op jit(solution)/shard_map/ppermute | solution.py:19
  140.6 31.6 %all-to-all-start = ((bf16[4,2,65536]{2,1,0:T(2,128)(2,1)}), bf16[4,2,65536]{2,1,0:T(2,128)(2,1)S(1)}, u32[]{:S(2)}, u32[]{:S(2)}) async-start(bf16[4,2,65536]{2,1,0:T(2,128)(2,1)} %reshape.60), calls=%async_computation | async-start | bytes 2097152 | tf_op jit(solution)/shard_map/all_to_all | solution.py:66
  146.9 161.6 %reduce-scatter.2.cloned.1.call-start = ((), (), s32[]{:S(2)}) async-start(), calls=%async_computation.2 | async-start | bytes 10485760 | tf_op jit(solution)/shard_map/reduce_scatter | solution.py:100
  183.5 1.4 copy-start.1
  185.0 7.9 %collective-permute-start = (bf16[1,64,1024]{2,1,0:T(8,128)(2,1)S(1)}, bf16[1,64,1024]{2,1,0:T(8,128)(2,1)S(1)}, u32[]{:S(2)}, u32[]{:S(2)}) collective-permute-start(bf16[1,64,1024]{2,1,0:T(8,128)(2,1)S(1)} %copy.32), channel_id=1, source_target_pairs={{0,4},{4,8},{8,12},{12,0},{1,5},{5,9},{9,13},{13,1},{2,6},{6,10},{... | collective-permute-start | bytes 393224 | tf_op jit(solution)/shard_map/while/body/eval_jaxpr/ppermute | solution.py:31
  188.1 9.3 %collective-permute-start.1 = (f32[1,64,1024]{2,1,0:T(8,128)S(1)}, f32[1,64,1024]{2,1,0:T(8,128)S(1)}, u32[]{:S(2)}, u32[]{:S(2)}) collective-permute-start(f32[1,64,1024]{2,1,0:T(8,128)S(1)} %fusion.44), channel_id=1, source_target_pairs={{0,4},{4,8},{8,12},{12,0},{1,5},{5,9},{9,13},{13,1},{2,6},{6,10},{... | collective-permute-start | bytes 786440 | tf_op jit(solution)/shard_map/while/body/eval_jaxpr/ppermute | solution.py:31
  197.4 11.2 %collective-permute-start = (bf16[1,64,1024]{2,1,0:T(8,128)(2,1)S(1)}, bf16[1,64,1024]{2,1,0:T(8,128)(2,1)S(1)}, u32[]{:S(2)}, u32[]{:S(2)}) collective-permute-start(bf16[1,64,1024]{2,1,0:T(8,128)(2,1)S(1)} %copy.32), channel_id=1, source_target_pairs={{0,4},{4,8},{8,12},{12,0},{1,5},{5,9},{9,13},{13,1},{2,6},{6,10},{... | collective-permute-start | bytes 393224 | tf_op jit(solution)/shard_map/while/body/eval_jaxpr/ppermute | solution.py:31
  200.6 9.3 %collective-permute-start.1 = (f32[1,64,1024]{2,1,0:T(8,128)S(1)}, f32[1,64,1024]{2,1,0:T(8,128)S(1)}, u32[]{:S(2)}, u32[]{:S(2)}) collective-permute-start(f32[1,64,1024]{2,1,0:T(8,128)S(1)} %fusion.44), channel_id=1, source_target_pairs={{0,4},{4,8},{8,12},{12,0},{1,5},{5,9},{9,13},{13,1},{2,6},{6,10},{... | collective-permute-start | bytes 786440 | tf_op jit(solution)/shard_map/while/body/eval_jaxpr/ppermute | solution.py:31
  209.9 14.6 %collective-permute-start = (bf16[1,64,1024]{2,1,0:T(8,128)(2,1)S(1)}, bf16[1,64,1024]{2,1,0:T(8,128)(2,1)S(1)}, u32[]{:S(2)}, u32[]{:S(2)}) collective-permute-start(bf16[1,64,1024]{2,1,0:T(8,128)(2,1)S(1)} %copy.32), channel_id=1, source_target_pairs={{0,4},{4,8},{8,12},{12,0},{1,5},{5,9},{9,13},{13,1},{2,6},{6,10},{... | collective-permute-start | bytes 393224 | tf_op jit(solution)/shard_map/while/body/eval_jaxpr/ppermute | solution.py:31
  214.2 10.3 %collective-permute-start.1 = (f32[1,64,1024]{2,1,0:T(8,128)S(1)}, f32[1,64,1024]{2,1,0:T(8,128)S(1)}, u32[]{:S(2)}, u32[]{:S(2)}) collective-permute-start(f32[1,64,1024]{2,1,0:T(8,128)S(1)} %fusion.44), channel_id=1, source_target_pairs={{0,4},{4,8},{8,12},{12,0},{1,5},{5,9},{9,13},{13,1},{2,6},{6,10},{... | collective-permute-start | bytes 786440 | tf_op jit(solution)/shard_map/while/body/eval_jaxpr/ppermute | solution.py:31
  224.5 12.4 %collective-permute-start = (bf16[1,64,1024]{2,1,0:T(8,128)(2,1)S(1)}, bf16[1,64,1024]{2,1,0:T(8,128)(2,1)S(1)}, u32[]{:S(2)}, u32[]{:S(2)}) collective-permute-start(bf16[1,64,1024]{2,1,0:T(8,128)(2,1)S(1)} %copy.32), channel_id=1, source_target_pairs={{0,4},{4,8},{8,12},{12,0},{1,5},{5,9},{9,13},{13,1},{2,6},{6,10},{... | collective-permute-start | bytes 393224 | tf_op jit(solution)/shard_map/while/body/eval_jaxpr/ppermute | solution.py:31
  227.6 9.3 %collective-permute-start.1 = (f32[1,64,1024]{2,1,0:T(8,128)S(1)}, f32[1,64,1024]{2,1,0:T(8,128)S(1)}, u32[]{:S(2)}, u32[]{:S(2)}) collective-permute-start(f32[1,64,1024]{2,1,0:T(8,128)S(1)} %fusion.44), channel_id=1, source_target_pairs={{0,4},{4,8},{8,12},{12,0},{1,5},{5,9},{9,13},{13,1},{2,6},{6,10},{... | collective-permute-start | bytes 786440 | tf_op jit(solution)/shard_map/while/body/eval_jaxpr/ppermute | solution.py:31
Sparse Core Ops, SparseCore 0:
  237.1 71.4 reduce-scatter.1
where the time goes:
time: 320 us; the launch traced here: 319 us
  waiting for transfers between devices  142 us (44%)
  other arithmetic  70.3 us (22%)
  matrix products  40.3 us (13%)
  local copies, waits for them, and re-layouts  28.6 us (9%)
  starting transfers between devices  22.6 us (7%)
  between operations  14.2 us (4%)
    reduce_scatter x1, waiting for transfers between devices, shards(): lax.psum_scatter(query_total, ('sub', 'pair'), scatter_dimension=0, tiled...  70.9 us
    unnamed x3, other arithmetic  45.5 us
    ppermute x2, waiting for transfers between devices, extended(): lax.ppermute(tail, axis, [(i, (i + 1) % count) for i in range(ends)])  40.4 us
    dot_general x4, matrix products, project(): lax.dot_general(block, feat_flat, (((0,), (0,)), ((), ())), preferred_ele...  28.1 us
    all_to_all x1, waiting for transfers between devices, shards(): lax.all_to_all(corr_grad, 'blk', split_axis=2, concat_axis=0, tiled=True)  25.3 us
    dot_general x4, matrix products, project(): jnp.dot(block, query_feats, preferred_element_type=jnp.float32)  12.1 us
    convert_element_type x1, other arithmetic, shards(): corr_grad = (query_pass(grad_volume, query_kernel) + support_pass(rimmed,...  11.4 us
    add x1, other arithmetic, query_pass(): total + kernel[row_shift, col_shift] * padded[:, :, row_shift:row_shift +...  9.43 us
  transfers between devices with their start and end apart: 14, of which 5 were waited for; matrix products, arithmetic and copies ran while one was open for 18% of the time, Pallas kernels for 0%

commit v1 on v0

--- a/solution.py
+++ b/solution.py
@@ -63,7 +63,10 @@
         query_pass(grad_volume, query_kernel)
         + support_pass(rimmed, support_kernel, planes, columns)
     ).astype(jnp.bfloat16)
-    moved = lax.all_to_all(corr_grad, "blk", split_axis=2, concat_axis=0, tiled=True)
+    moved = jnp.concatenate(
+        lax.all_to_all(jnp.stack(jnp.split(corr_grad, lax.axis_size("blk"), axis=2)), "blk", 0, 0),
+        axis=0,
+    )
     cycle_size = lax.axis_size("blk")
     own_index = lax.axis_index("blk")
     tile_len = moved.shape[2]

time: 320 us -> 255 us (0.80)
  other arithmetic: 70.3 us -> 26.1 us
  local copies, waits for them, and re-layouts: 28.6 us -> 6.58 us
    unnamed x3 -> x2, other arithmetic: 45.5 us -> 0.24 us
    all_to_all x2 -> x0, local copies, waits for them, and re-layouts: 8.96 us -> none  [shards(): lax.all_to_all(corr_grad, 'blk', split_axis=2, concat_axis=0, tiled=True)]
    unnamed x16 -> x10, local copies, waits for them, and re-layouts: 7.52 us -> 0.46 us
    convert_element_type x1 -> x0, local copies, waits for them, and re-layouts: 6.78 us -> none  [shards(): corr_grad = (query_pass(grad_volume, query_kernel) + support_pass(rimmed,...]
  transfers between devices with their start and end apart: 14 -> 14, of which waited for: 5 -> 5; matrix products, arithmetic and copies ran while one was open for 18% -> 22% of each run, Pallas kernels for 0% -> 0%
where the time goes in v1:
time: 255 us; the launch traced here: 254 us
  waiting for transfers between devices  145 us (57%)
  matrix products  40.3 us (16%)
  other arithmetic  26.1 us (10%)
  starting transfers between devices  21.8 us (9%)
  between operations  14.2 us (6%)
  local copies, waits for them, and re-layouts  6.58 us (3%)
    reduce_scatter x1, waiting for transfers between devices, shards(): lax.psum_scatter(query_total, ('sub', 'pair'), scatter_dimension=0, tiled...  70.9 us
    ppermute x2, waiting for transfers between devices, extended(): lax.ppermute(tail, axis, [(i, (i + 1) % count) for i in range(ends)])  40.5 us
    dot_general x4, matrix products, project(): lax.dot_general(block, feat_flat, (((0,), (0,)), ((), ())), preferred_ele...  28.2 us
    all_to_all x1, waiting for transfers between devices, shards(): lax.all_to_all(jnp.stack(jnp.split(corr_grad, lax.axis_size('blk'), axis=...  27 us
    dot_general x4, matrix products, project(): jnp.dot(block, query_feats, preferred_element_type=jnp.float32)  12.1 us
    convert_element_type x1, other arithmetic, shards(): corr_grad = (query_pass(grad_volume, query_kernel) + support_pass(rimmed,...  11.2 us
    add x1, other arithmetic, query_pass(): total + kernel[row_shift, col_shift] * padded[:, :, row_shift:row_shift +...  9.56 us
    all_to_all x1, starting transfers between devices, shards(): lax.all_to_all(jnp.stack(jnp.split(corr_grad, lax.axis_size('blk'), axis=...  6.94 us
  transfers between devices with their start and end apart: 14, of which 5 were waited for; matrix products, arithmetic and copies ran while one was open for 22% of the time, Pallas kernels for 0%

profile of v1, /device:TPU:0, one launch (start us, length us, event | category | flops | bytes accessed | tf_op | source)
XLA Modules:
  0.0 253.7 jit_solution(7374749532282906180)
XLA Ops:
  7.2 0.0 copy-start.3
  7.2 5.0 %collective-permute-start.2 = (bf16[1,64,8192]{2,1,0:T(8,128)(2,1)}, bf16[1,64,8192]{2,1,0:T(8,128)(2,1)S(1)}, u32[]{:S(2)}, u32[]{:S(2)}) collective-permute-start(bf16[1,64,8192]{2,1,0:T(8,128)(2,1)} %param.7), channel_id=1, source_target_pairs={{0,2},{2,4},{4,6},{6,8},{8,10},{10,12},{12,14},{1,3},{3,5},{5,7},{... | collective-permute-start | bytes 3145736 | tf_op jit(solution)/shard_map/ppermute | solution.py:19
  12.2 1.3 collective-permute-start.3
  13.5 1.7 fusion.33
  15.2 1.7 fusion.32
  16.9 40.5 %collective-permute-done.2 = bf16[1,64,8192]{2,1,0:T(8,128)(2,1)S(1)} collective-permute-done((bf16[1,64,8192]{2,1,0:T(8,128)(2,1)}, bf16[1,64,8192]{2,1,0:T(8,128)(2,1)S(1)}, u32[]{:S(2)}, u32[]{:S(2)}) %collective-permute-start.2) | collective-permute-done | bytes 1048608 | tf_op jit(solution)/shard_map/ppermute | solution.py:19
  57.3 0.1 constant_dynamic-update-slice_fusion.2
  57.4 0.0 copy-done.3
  57.4 0.2 constant_dynamic-update-slice_fusion.1
  57.7 0.0 collective-permute-done.3
  57.7 0.0 copy-start.2
  57.7 0.1 constant_dynamic-update-slice_fusion
  57.8 0.0 copy-start
  57.8 1.0 fusion.31
  58.8 1.3 collective-permute-start.4
  60.1 1.3 collective-permute-start.5
  61.4 0.4 copy.7
  61.8 0.0 copy-done.2
  61.8 0.0 copy-done
  61.8 9.6 %fusion.23 = f32[1,64,64,128]{3,2,1,0:T(8,128)S(1)} fusion(f32[1,64,64,128]{3,2,1,0:T(8,128)S(1)} %bitcast.56, f32[]{:T(128)} %bitcast.8, f32[]{:T(128)} %bitcast.7, f32[]{:T(128)} %bitcast.6, f32[]{:T(128)} %bitcast.5, f32[]{:T(128)} %bitcast.4, f32[]{:T(128)} %bitcast.3, f32[]{:T(128)} %bitcast.2, f32[]{:T(128)} %bitcast.1, f32[]{:T(128)} %bitcast), kind=kLoop, calls=%fused_computation.35 | loop fusion | flops 8912896 | bytes 4194340 | tf_op jit(solution)/shard_map/add | solution.py:42
  71.4 1.5 reshape.54
  72.9 0.0 collective-permute-done.4
  72.9 0.0 collective-permute-done.5
  72.9 11.2 %fusion.14 = bf16[1,64,8192]{2,1,0:T(8,128)(2,1)S(1)} fusion(f32[1,64,8192]{2,1,0:T(8,128)} %reshape.54, bf16[1,64,8192]{2,1,0:T(8,128)(2,1)} %param.7, bf16[1,64,8192]{2,1,0:T(8,128)(2,1)} %copy-done.2, bf16[1,64,8192]{2,1,0:T(8,128)(2,1)S(1)} %collective-permute-done.2, bf16[3,1,8192]{2,1,0:T(2,128)(2,1)S(1)} %collective-permute-done.5, ...), kind=kLoop, calls=%fused_computation.26 | loop fusion | flops 24117248 | bytes 9535524 | tf_op jit(solution)/shard_map/convert_element_type | solution.py:65
  84.1 0.1 slice_bitcast_fusion.3
  84.2 0.0 copy-start.1
  84.2 1.1 pad_maximum_fusion.2
  85.3 6.9 %all-to-all-start = ((bf16[4,1,64,2048]{3,2,1,0:T(8,128)(2,1)}), bf16[4,1,64,2048]{3,2,1,0:T(8,128)(2,1)S(1)}, u32[]{:S(2)}, u32[]{:S(2)}) async-start(bf16[4,1,64,2048]{3,2,1,0:T(8,128)(2,1)} %pad_maximum_fusion.2), calls=%async_computation | async-start | bytes 2097152 | tf_op jit(solution)/shard_map/all_to_all | solution.py:67
  92.3 0.0 reduce-scatter.2.cloned.1.call-start
  92.3 27.0 %all-to-all-done = bf16[4,1,64,2048]{3,2,1,0:T(8,128)(2,1)S(1)} async-done(((bf16[4,1,64,2048]{3,2,1,0:T(8,128)(2,1)}), bf16[4,1,64,2048]{3,2,1,0:T(8,128)(2,1)S(1)}, u32[]{:S(2)}, u32[]{:S(2)}) %all-to-all-start) | async-done | bytes 1048608 | tf_op jit(solution)/shard_map/all_to_all | solution.py:67
  119.3 0.0 copy-done.1
  119.3 52.7 %while.20 = (s32[]{:T(128)}, f32[2048,1024]{1,0:T(8,128)}, bf16[1,64,1024]{2,1,0:T(8,128)(2,1)S(1)}, f32[1,64,1024]{2,1,0:T(8,128)S(1)}, s32[]{:T(128)}, /*index...) while((s32[]{:T(128)}, f32[2048,1024]{1,0:T(8,128)}, ...), condition=%wide.region_1.2_spmd.clone, body=%wide.region_0.1_spmd.clone.sunk | while | flops 541130752 | bytes 23986536 | solution.py:101
  119.4 0.1 collective-permute-start
  119.4 3.0 %fusion.44 = f32[1,64,1024]{2,1,0:T(8,128)S(1)} fusion(f32[1,64,1024]{2,1,0:T(8,128)S(1)} %get-tuple-element.303, bf16[2048,1024]{1,0:T(8,128)(2,1)} %get-tuple-element.317, bf16[4,1,64,2048]{3,2,1,0:T(8,128)(2,1)S(1)} %get-tuple-element.316, s32[]{:T(128)S(6)} %select_n.36), kind=kOutput, calls=%fused_computation.2.clone.1 | convolution fusion | flops 268500992 | bytes 4980740 | tf_op jit(solution)/shard_map/while/body/eval_jaxpr/dot_general | solution.py:84
  122.5 0.2 collective-permute-start.1
  122.7 4.5 %select_add_fusion.2 = f32[2048,1024]{1,0:T(8,128)} fusion(f32[2048,1024]{1,0:T(8,128)} %get-tuple-element.301, pred[]{:T(512)S(6)} %compare.5, bf16[4,1,64,2048]{3,2,1,0:T(8,128)(2,1)S(1)} %get-tuple-element.316, s32[]{:T(128)S(6)} %select_n.36, bf16[1,64,1024]{2,1,0:T(8,128)(2,1)S(1)} %copy.16), kind=kOutput, calls=%fused_computation.clone.1 | convolution fusion | flops 272629760 | bytes 17170436 | tf_op jit(solution)/shard_map/while/body/eval_jaxpr/dot_general | solution.py:81
  127.2 0.0 collective-permute-done
  127.2 5.3 %collective-permute-done.1 = f32[1,64,1024]{2,1,0:T(8,128)S(1)} collective-permute-done((f32[1,64,1024]{2,1,0:T(8,128)S(1)}, f32[1,64,1024]{2,1,0:T(8,128)S(1)}, u32[]{:S(2)}, u32[]{:S(2)}) %collective-permute-start.1) | collective-permute-done | bytes 262176 | tf_op jit(solution)/shard_map/while/body/eval_jaxpr/ppermute | solution.py:31
  132.6 0.1 collective-permute-start
  132.6 3.0 %fusion.44 = f32[1,64,1024]{2,1,0:T(8,128)S(1)} fusion(f32[1,64,1024]{2,1,0:T(8,128)S(1)} %get-tuple-element.303, bf16[2048,1024]{1,0:T(8,128)(2,1)} %get-tuple-element.317, bf16[4,1,64,2048]{3,2,1,0:T(8,128)(2,1)S(1)} %get-tuple-element.316, s32[]{:T(128)S(6)} %select_n.36), kind=kOutput, calls=%fused_computation.2.clone.1 | convolution fusion | flops 268500992 | bytes 4980740 | tf_op jit(solution)/shard_map/while/body/eval_jaxpr/dot_general | solution.py:84
  135.7 0.5 collective-permute-start.1
  136.2 7.9 %select_add_fusion.2 = f32[2048,1024]{1,0:T(8,128)} fusion(f32[2048,1024]{1,0:T(8,128)} %get-tuple-element.301, pred[]{:T(512)S(6)} %compare.5, bf16[4,1,64,2048]{3,2,1,0:T(8,128)(2,1)S(1)} %get-tuple-element.316, s32[]{:T(128)S(6)} %select_n.36, bf16[1,64,1024]{2,1,0:T(8,128)(2,1)S(1)} %copy.16), kind=kOutput, calls=%fused_computation.clone.1 | convolution fusion | flops 272629760 | bytes 17170436 | tf_op jit(solution)/shard_map/while/body/eval_jaxpr/dot_general | solution.py:81
  144.1 0.0 collective-permute-done
  144.1 0.9 collective-permute-done.1
  145.0 1.5 collective-permute-start
  146.5 3.0 %fusion.44 = f32[1,64,1024]{2,1,0:T(8,128)S(1)} fusion(f32[1,64,1024]{2,1,0:T(8,128)S(1)} %get-tuple-element.303, bf16[2048,1024]{1,0:T(8,128)(2,1)} %get-tuple-element.317, bf16[4,1,64,2048]{3,2,1,0:T(8,128)(2,1)S(1)} %get-tuple-element.316, s32[]{:T(128)S(6)} %select_n.36), kind=kOutput, calls=%fused_computation.2.clone.1 | convolution fusion | flops 268500992 | bytes 4980740 | tf_op jit(solution)/shard_map/while/body/eval_jaxpr/dot_general | solution.py:84
  149.5 2.2 collective-permute-start.1
  151.7 7.9 %select_add_fusion.2 = f32[2048,1024]{1,0:T(8,128)} fusion(f32[2048,1024]{1,0:T(8,128)} %get-tuple-element.301, pred[]{:T(512)S(6)} %compare.5, bf16[4,1,64,2048]{3,2,1,0:T(8,128)(2,1)S(1)} %get-tuple-element.316, s32[]{:T(128)S(6)} %select_n.36, bf16[1,64,1024]{2,1,0:T(8,128)(2,1)S(1)} %copy.16), kind=kOutput, calls=%fused_computation.clone.1 | convolution fusion | flops 272629760 | bytes 17170436 | tf_op jit(solution)/shard_map/while/body/eval_jaxpr/dot_general | solution.py:81
  159.6 0.0 collective-permute-done
  159.6 0.0 collective-permute-done.1
  159.6 0.1 collective-permute-start
  159.7 3.0 %fusion.44 = f32[1,64,1024]{2,1,0:T(8,128)S(1)} fusion(f32[1,64,1024]{2,1,0:T(8,128)S(1)} %get-tuple-element.303, bf16[2048,1024]{1,0:T(8,128)(2,1)} %get-tuple-element.317, bf16[4,1,64,2048]{3,2,1,0:T(8,128)(2,1)S(1)} %get-tuple-element.316, s32[]{:T(128)S(6)} %select_n.36), kind=kOutput, calls=%fused_computation.2.clone.1 | convolution fusion | flops 268500992 | bytes 4980740 | tf_op jit(solution)/shard_map/while/body/eval_jaxpr/dot_general | solution.py:84
  162.8 1.4 collective-permute-start.1
  164.2 7.9 %select_add_fusion.2 = f32[2048,1024]{1,0:T(8,128)} fusion(f32[2048,1024]{1,0:T(8,128)} %get-tuple-element.301, pred[]{:T(512)S(6)} %compare.5, bf16[4,1,64,2048]{3,2,1,0:T(8,128)(2,1)S(1)} %get-tuple-element.316, s32[]{:T(128)S(6)} %select_n.36, bf16[1,64,1024]{2,1,0:T(8,128)(2,1)S(1)} %copy.16), kind=kOutput, calls=%fused_computation.clone.1 | convolution fusion | flops 272629760 | bytes 17170436 | tf_op jit(solution)/shard_map/while/body/eval_jaxpr/dot_general | solution.py:81
  172.0 0.0 collective-permute-done
  172.1 0.0 collective-permute-done.1
  172.1 0.0 reduce-scatter.2.cloned.1.call-update
  172.1 0.7 broadcast_multiply_fusion.1
  172.8 70.9 %reduce-scatter.2.cloned.1.call-done = f32[512,1024]{1,0:T(8,128)} async-done(((f32[2048,1024]{1,0:T(8,128)}), f32[512,1024]{1,0:T(8,128)}) %reduce-scatter.2.cloned.1.call-update) | async-done | bytes 2097168 | tf_op jit(solution)/shard_map/reduce_scatter | solution.py:103
  243.7 3.2 %broadcast_multiply_fusion = f32[512,1024]{1,0:T(8,128)} fusion(f32[512,1024]{1,0:T(8,128)} %reduce-scatter.2.cloned.1.call-done), kind=kLoop, calls=%fused_computation.46 | loop fusion | flops 524288 | bytes 4194304 | tf_op jit(solution)/shard_map/mul | solution.py:103
  (6 shorter events, 0.1 us)
Async XLA Ops:
  7.2 50.3 %copy-start.3 = (bf16[1,64,8192]{2,1,0:T(8,128)(2,1)S(1)}, bf16[1,64,8192]{2,1,0:T(8,128)(2,1)}, u32[]{:S(2)}) copy-start(bf16[1,64,8192]{2,1,0:T(8,128)(2,1)} %param.7) | copy-start | bytes 3145732
  7.2 50.2 %collective-permute-start.2 = (bf16[1,64,8192]{2,1,0:T(8,128)(2,1)}, bf16[1,64,8192]{2,1,0:T(8,128)(2,1)S(1)}, u32[]{:S(2)}, u32[]{:S(2)}) collective-permute-start(bf16[1,64,8192]{2,1,0:T(8,128)(2,1)} %param.7), channel_id=1, source_target_pairs={{0,2},{2,4},{4,6},{6,8},{8,10},{10,12},{12,14},{1,3},{3,5},{5,7},{... | collective-permute-start | bytes 3145736 | tf_op jit(solution)/shard_map/ppermute | solution.py:19
  12.2 45.5 %collective-permute-start.3 = (bf16[1,64,8192]{2,1,0:T(8,128)(2,1)}, bf16[1,64,8192]{2,1,0:T(8,128)(2,1)S(1)}, u32[]{:S(2)}, u32[]{:S(2)}) collective-permute-start(bf16[1,64,8192]{2,1,0:T(8,128)(2,1)} %param.7), channel_id=1, source_target_pairs={{2,0},{4,2},{6,4},{8,6},{10,8},{12,10},{14,12},{3,1},{5,3},{7,5},{... | collective-permute-start | bytes 3145736 | tf_op jit(solution)/shard_map/ppermute | solution.py:21
  57.7 4.1 %copy-start.2 = (bf16[1,64,8192]{2,1,0:T(8,128)(2,1)}, bf16[1,64,8192]{2,1,0:T(8,128)(2,1)S(1)}, u32[]{:S(2)}) copy-start(bf16[1,64,8192]{2,1,0:T(8,128)(2,1)S(1)} %collective-permute-done.3) | copy-start | bytes 3145732
  57.8 4.0 %copy-start = (bf16[3,64,8192]{2,1,0:T(8,128)(2,1)}, bf16[3,64,8192]{2,1,0:T(8,128)(2,1)S(1)}, u32[]{:S(2)}) copy-start(bf16[3,64,8192]{2,1,0:T(8,128)(2,1)S(1)} %constant_dynamic-update-slice_fusion) | copy-start | bytes 9437188
  58.8 14.1 %collective-permute-start.4 = (bf16[3,1,8192]{2,1,0:T(2,128)(2,1)}, bf16[3,1,8192]{2,1,0:T(2,128)(2,1)S(1)}, u32[]{:S(2)}, u32[]{:S(2)}) collective-permute-start(bf16[3,1,8192]{2,1,0:T(2,128)(2,1)} %get-tuple-element.220), channel_id=1, source_target_pairs={{0,1},{2,3},{4,5},{6,7},{8,9},{10,11},{12,13},{14,15},{16,17},{18,... | collective-permute-start | bytes 147464 | tf_op jit(solution)/shard_map/ppermute | solution.py:19
  60.1 12.8 %collective-permute-start.5 = (bf16[3,1,8192]{2,1,0:T(2,128)(2,1)S(1)}, bf16[3,1,8192]{2,1,0:T(2,128)(2,1)S(1)}, u32[]{:S(2)}, u32[]{:S(2)}) collective-permute-start(bf16[3,1,8192]{2,1,0:T(2,128)(2,1)S(1)} %get-tuple-element.221), channel_id=1, source_target_pairs={{1,0},{3,2},{5,4},{7,6},{9,8},{11,10},{13,12},{15,14},{17,16},{19,... | collective-permute-start | bytes 147464 | tf_op jit(solution)/shard_map/ppermute | solution.py:21
  84.2 35.1 %copy-start.1 = (bf16[1,64,1024]{2,1,0:T(8,128)(2,1)S(1)}, bf16[1,64,1024]{2,1,0:T(8,128)(2,1)}, u32[]{:S(2)}) copy-start(bf16[1,64,1024]{2,1,0:T(8,128)(2,1)} %param.9) | copy-start | bytes 393220
  85.3 34.0 %all-to-all-start = ((bf16[4,1,64,2048]{3,2,1,0:T(8,128)(2,1)}), bf16[4,1,64,2048]{3,2,1,0:T(8,128)(2,1)S(1)}, u32[]{:S(2)}, u32[]{:S(2)}) async-start(bf16[4,1,64,2048]{3,2,1,0:T(8,128)(2,1)} %pad_maximum_fusion.2), calls=%async_computation | async-start | bytes 2097152 | tf_op jit(solution)/shard_map/all_to_all | solution.py:67
  92.3 151.4 %reduce-scatter.2.cloned.1.call-start = ((), (), s32[]{:S(2)}) async-start(), calls=%async_computation.2 | async-start | bytes 10485760 | tf_op jit(solution)/shard_map/reduce_scatter | solution.py:103
  119.4 7.9 %collective-permute-start = (bf16[1,64,1024]{2,1,0:T(8,128)(2,1)S(1)}, bf16[1,64,1024]{2,1,0:T(8,128)(2,1)S(1)}, u32[]{:S(2)}, u32[]{:S(2)}) collective-permute-start(bf16[1,64,1024]{2,1,0:T(8,128)(2,1)S(1)} %copy.16), channel_id=1, source_target_pairs={{0,4},{4,8},{8,12},{12,0},{1,5},{5,9},{9,13},{13,1},{2,6},{6,10},{... | collective-permute-start | bytes 393224 | tf_op jit(solution)/shard_map/while/body/eval_jaxpr/ppermute | solution.py:31
  122.5 10.1 %collective-permute-start.1 = (f32[1,64,1024]{2,1,0:T(8,128)S(1)}, f32[1,64,1024]{2,1,0:T(8,128)S(1)}, u32[]{:S(2)}, u32[]{:S(2)}) collective-permute-start(f32[1,64,1024]{2,1,0:T(8,128)S(1)} %fusion.44), channel_id=1, source_target_pairs={{0,4},{4,8},{8,12},{12,0},{1,5},{5,9},{9,13},{13,1},{2,6},{6,10},{... | collective-permute-start | bytes 786440 | tf_op jit(solution)/shard_map/while/body/eval_jaxpr/ppermute | solution.py:31
  132.6 11.5 %collective-permute-start = (bf16[1,64,1024]{2,1,0:T(8,128)(2,1)S(1)}, bf16[1,64,1024]{2,1,0:T(8,128)(2,1)S(1)}, u32[]{:S(2)}, u32[]{:S(2)}) collective-permute-start(bf16[1,64,1024]{2,1,0:T(8,128)(2,1)S(1)} %copy.16), channel_id=1, source_target_pairs={{0,4},{4,8},{8,12},{12,0},{1,5},{5,9},{9,13},{13,1},{2,6},{6,10},{... | collective-permute-start | bytes 393224 | tf_op jit(solution)/shard_map/while/body/eval_jaxpr/ppermute | solution.py:31
  135.7 9.3 %collective-permute-start.1 = (f32[1,64,1024]{2,1,0:T(8,128)S(1)}, f32[1,64,1024]{2,1,0:T(8,128)S(1)}, u32[]{:S(2)}, u32[]{:S(2)}) collective-permute-start(f32[1,64,1024]{2,1,0:T(8,128)S(1)} %fusion.44), channel_id=1, source_target_pairs={{0,4},{4,8},{8,12},{12,0},{1,5},{5,9},{9,13},{13,1},{2,6},{6,10},{... | collective-permute-start | bytes 786440 | tf_op jit(solution)/shard_map/while/body/eval_jaxpr/ppermute | solution.py:31
  145.0 14.6 %collective-permute-start = (bf16[1,64,1024]{2,1,0:T(8,128)(2,1)S(1)}, bf16[1,64,1024]{2,1,0:T(8,128)(2,1)S(1)}, u32[]{:S(2)}, u32[]{:S(2)}) collective-permute-start(bf16[1,64,1024]{2,1,0:T(8,128)(2,1)S(1)} %copy.16), channel_id=1, source_target_pairs={{0,4},{4,8},{8,12},{12,0},{1,5},{5,9},{9,13},{13,1},{2,6},{6,10},{... | collective-permute-start | bytes 393224 | tf_op jit(solution)/shard_map/while/body/eval_jaxpr/ppermute | solution.py:31
  149.5 10.1 %collective-permute-start.1 = (f32[1,64,1024]{2,1,0:T(8,128)S(1)}, f32[1,64,1024]{2,1,0:T(8,128)S(1)}, u32[]{:S(2)}, u32[]{:S(2)}) collective-permute-start(f32[1,64,1024]{2,1,0:T(8,128)S(1)} %fusion.44), channel_id=1, source_target_pairs={{0,4},{4,8},{8,12},{12,0},{1,5},{5,9},{9,13},{13,1},{2,6},{6,10},{... | collective-permute-start | bytes 786440 | tf_op jit(solution)/shard_map/while/body/eval_jaxpr/ppermute | solution.py:31
  159.6 12.4 %collective-permute-start = (bf16[1,64,1024]{2,1,0:T(8,128)(2,1)S(1)}, bf16[1,64,1024]{2,1,0:T(8,128)(2,1)S(1)}, u32[]{:S(2)}, u32[]{:S(2)}) collective-permute-start(bf16[1,64,1024]{2,1,0:T(8,128)(2,1)S(1)} %copy.16), channel_id=1, source_target_pairs={{0,4},{4,8},{8,12},{12,0},{1,5},{5,9},{9,13},{13,1},{2,6},{6,10},{... | collective-permute-start | bytes 393224 | tf_op jit(solution)/shard_map/while/body/eval_jaxpr/ppermute | solution.py:31
  162.8 9.3 %collective-permute-start.1 = (f32[1,64,1024]{2,1,0:T(8,128)S(1)}, f32[1,64,1024]{2,1,0:T(8,128)S(1)}, u32[]{:S(2)}, u32[]{:S(2)}) collective-permute-start(f32[1,64,1024]{2,1,0:T(8,128)S(1)} %fusion.44), channel_id=1, source_target_pairs={{0,4},{4,8},{8,12},{12,0},{1,5},{5,9},{9,13},{13,1},{2,6},{6,10},{... | collective-permute-start | bytes 786440 | tf_op jit(solution)/shard_map/while/body/eval_jaxpr/ppermute | solution.py:31
Sparse Core Ops, SparseCore 0:
  172.2 71.4 reduce-scatter.1
